TPU v7x, 32 devices: a whole 2x2x4 slice. The times are simulated.
32 devices in a mesh: dp: 16 (over z, y, x), tensor: 2 (over core).
Axes of the slice: x: 2, y: 2, z: 4, core: 2. Of those that a mesh axis runs over, the one named last changes fastest.
Arguments:
- tokens: bfloat16 [2, 8192, 768], P(None, 'dp'), may hold values from -6 to 6
- seg_doc: int32 [2, 64], replicated, may hold values from 0 to 15, as said below
- doc_len: int32 [2, 16], replicated, may hold values from 1 to 1024, as said below
- w_qkv: bfloat16 [2, 3, 768, 768], P(None, None, None, 'tensor'), may hold values from -0.21875 to 0.21875
- b_qv: float32 [2, 2, 768], P(None, None, 'tensor'), may hold values from -3 to 3
- w_out: bfloat16 [2, 768, 768], P(None, 'tensor'), may hold values from -0.625 to 0.625
- w_up: bfloat16 [2, 768, 3072], P(None, None, 'tensor'), may hold values from -0.21875 to 0.21875
- b_up: float32 [2, 3072], P(None, 'tensor'), may hold values from -3 to 3
- w_down: bfloat16 [2, 3072, 768], P(None, 'tensor'), may hold values from -0.109375 to 0.109375
- norm_gain: float32 [2, 2, 768], replicated, may hold values from 0.25 to 1.75
- bias_terms: float32 [2, 4, 768], replicated, may hold values from -3 to 3
- seg_pos: float32 [8, 768], replicated, may hold values from -3 to 3
- cotangent: bfloat16 [2, 8192, 768], P(None, 'dp'), may hold values from -6 to 6
Outputs:
- encoded: bfloat16 [2, 8192, 768], P(None, 'dp')
- grad_tokens: float32 [2, 8192, 768], P(None, 'dp')
- grad_w_qkv: float32 [2, 3, 768, 768], P(None, None, 'dp', 'tensor')
- grad_b_qv: float32 [2, 2, 768], P(None, None, 'tensor')
- grad_w_out: float32 [2, 768, 768], P(None, 'tensor', 'dp')
- grad_w_up: float32 [2, 768, 3072], P(None, 'dp', 'tensor')
- grad_b_up: float32 [2, 3072], P(None, 'tensor')
- grad_w_down: float32 [2, 3072, 768], P(None, 'tensor', 'dp')
- grad_norm_gain: float32 [2, 2, 768], replicated
- grad_bias_terms: float32 [2, 4, 768], replicated
- grad_seg_pos: float32 [8, 768], replicated
Inputs may be any that keep to these rules, and one draw needn't show every extreme that they name: `seg_doc`: segment ids never fall along a micro-batch; every document 0 to 15 covers 1 to 8 consecutive segments. `doc_len`: A document of n segments has more than 128 * (n - 1) and at most 128 * n tokens; in every micro-batch one document has exactly 1024.
All inputs are finite; a program needn't handle non-finite values.
Results may differ from a plain program's by a relative error of at most 0.024.
Values may be sent and summed in bfloat16 or wider, within the bound.
A program may use at most 192 MiB of HBM per device.

v0:
```python
from functools import partial, reduce

import jax
import jax.numpy as jnp
from jax import lax
from jax.experimental import pallas as pl
from jax.experimental.pallas import tpu as pltpu
from jax.sharding import PartitionSpec as P

HEAD_DIM = 64
SEG = 128
MAXSEG = 8


norm_eps = 1e-05
masked_score = -1e30


def norm_rows(values, gain, shift):
    centre = values - jnp.mean(values, axis=-1, keepdims=True)
    spread = jnp.mean(centre * centre, axis=-1, keepdims=True)
    return centre * lax.rsqrt(spread + norm_eps) * gain + shift


def exact_gelu(values):
    return jax.nn.gelu(values, approximate=False)


def my_rows(values):
    part_rows = values.shape[0] // lax.axis_size("tensor")
    return lax.dynamic_slice_in_dim(values, lax.axis_index("tensor") * part_rows, part_rows, 0)


def attn_scores(queries, key_rows, key_mask, split_shape):
    raw = jnp.einsum(
        "glhd,gmhd->ghlm",
        queries.reshape(split_shape),
        key_rows.reshape(split_shape),
        preferred_element_type=jnp.float32,
    ) * HEAD_DIM ** (-0.5)
    return jnp.where(key_mask[:, None, None, :], raw, masked_score)


def layer_forward(inputs, key_mask, weights):
    w_qkv, b_qv, w_out, w_up, b_up, w_down, norm_gain, bias_terms = weights
    groups, span = key_mask.shape
    row_count = inputs.shape[0]
    local_width = w_qkv.shape[2]
    split_shape = (groups, span, local_width // HEAD_DIM, HEAD_DIM)
    inputs_b = inputs.astype(jnp.bfloat16)
    projected = jnp.einsum("rd,cde->cre", inputs_b, w_qkv, preferred_element_type=jnp.float32)
    queries = (projected[0] + b_qv[0]).astype(jnp.bfloat16)
    key_rows = projected[1].astype(jnp.bfloat16)
    value_rows = (projected[2] + b_qv[1]).astype(jnp.bfloat16)
    scores = attn_scores(queries, key_rows, key_mask, split_shape)
    row_max = jnp.max(scores, axis=-1, keepdims=True)
    log_total = row_max + jnp.log(jnp.sum(jnp.exp(scores - row_max), axis=-1, keepdims=True))
    attn_probs = jnp.exp(scores - log_total).astype(jnp.bfloat16)
    head_out = jnp.einsum(
        "ghlm,gmhd->glhd",
        attn_probs,
        value_rows.reshape(split_shape),
        preferred_element_type=jnp.float32,
    )
    head_out = head_out.reshape(row_count, local_width).astype(jnp.bfloat16)
    attn_part = (
        lax.psum_scatter(
            jnp.dot(head_out, w_out, preferred_element_type=jnp.float32),
            "tensor",
            scatter_dimension=0,
            tiled=True,
        )
        + bias_terms[0]
    )
    resid_one = lax.all_gather(my_rows(inputs) + attn_part, "tensor", axis=0, tiled=True)
    hidden = norm_rows(resid_one, norm_gain[0], bias_terms[2])
    hidden_b = hidden.astype(jnp.bfloat16)
    pre_act = jnp.dot(hidden_b, w_up, preferred_element_type=jnp.float32) + b_up
    active_b = exact_gelu(pre_act).astype(jnp.bfloat16)
    mlp_part = (
        lax.psum_scatter(
            jnp.dot(active_b, w_down, preferred_element_type=jnp.float32),
            "tensor",
            scatter_dimension=0,
            tiled=True,
        )
        + bias_terms[1]
    )
    resid_two = lax.all_gather(my_rows(hidden) + mlp_part, "tensor", axis=0, tiled=True)
    stored = (
        inputs_b,
        queries,
        key_rows,
        value_rows,
        log_total,
        head_out,
        resid_one,
        hidden_b,
        pre_act,
        active_b,
        resid_two,
    )
    return (norm_rows(resid_two, norm_gain[1], bias_terms[3]), stored)


def layer_backward(grad_out, key_mask, weights, stored):
    w_qkv, b_qv, w_out, w_up, b_up, w_down, norm_gain, bias_terms = weights
    (
        inputs_b,
        queries,
        key_rows,
        value_rows,
        log_total,
        head_out,
        resid_one,
        hidden_b,
        pre_act,
        active_b,
        resid_two,
    ) = stored
    groups, span = key_mask.shape
    row_count, local_width = queries.shape
    split_shape = (groups, span, local_width // HEAD_DIM, HEAD_DIM)
    forward_two, norm_two = jax.vjp(norm_rows, resid_two, norm_gain[1], bias_terms[3])
    grad_two, gain_two, shift_two = norm_two(grad_out)
    grad_mlp = grad_two.astype(jnp.bfloat16)
    grad_wdown = jnp.dot(active_b.T, grad_mlp, preferred_element_type=jnp.float32)
    grad_act = jnp.dot(grad_mlp, w_down.T, preferred_element_type=jnp.float32)
    forward_gelu, gelu_back = jax.vjp(exact_gelu, pre_act)
    grad_pre = gelu_back(grad_act)[0].astype(jnp.bfloat16)
    grad_wup = jnp.dot(hidden_b.T, grad_pre, preferred_element_type=jnp.float32)
    up_part = lax.psum_scatter(
        jnp.dot(grad_pre, w_up.T, preferred_element_type=jnp.float32),
        "tensor",
        scatter_dimension=0,
        tiled=True,
    )
    grad_hidden = lax.all_gather(my_rows(grad_two) + up_part, "tensor", axis=0, tiled=True)
    forward_one, norm_one = jax.vjp(norm_rows, resid_one, norm_gain[0], bias_terms[2])
    grad_one, gain_one, shift_one = norm_one(grad_hidden)
    grad_attn = grad_one.astype(jnp.bfloat16)
    grad_wout = jnp.dot(head_out.T, grad_attn, preferred_element_type=jnp.float32)
    grad_heads = (
        jnp.dot(grad_attn, w_out.T, preferred_element_type=jnp.float32)
        .astype(jnp.bfloat16)
        .reshape(split_shape)
    )
    scores = attn_scores(queries, key_rows, key_mask, split_shape)
    attn_probs = jnp.exp(scores - log_total)
    grad_probs = jnp.einsum(
        "glhd,gmhd->ghlm",
        grad_heads,
        value_rows.reshape(split_shape),
        preferred_element_type=jnp.float32,
    )
    grad_values = jnp.einsum(
        "ghlm,glhd->gmhd",
        attn_probs.astype(jnp.bfloat16),
        grad_heads,
        preferred_element_type=jnp.float32,
    )
    grad_scores = (
        attn_probs * (grad_probs - jnp.sum(attn_probs * grad_probs, axis=-1, keepdims=True))
    ).astype(jnp.bfloat16)
    inv_root = HEAD_DIM ** (-0.5)
    grad_queries = (
        jnp.einsum(
            "ghlm,gmhd->glhd",
            grad_scores,
            key_rows.reshape(split_shape),
            preferred_element_type=jnp.float32,
        )
        * inv_root
    )
    grad_keys = (
        jnp.einsum(
            "ghlm,glhd->gmhd",
            grad_scores,
            queries.reshape(split_shape),
            preferred_element_type=jnp.float32,
        )
        * inv_root
    )
    grad_qkv = (
        jnp.stack([grad_queries, grad_keys, grad_values])
        .reshape(3, row_count, local_width)
        .astype(jnp.bfloat16)
    )
    grad_wqkv = jnp.einsum("rd,cre->cde", inputs_b, grad_qkv, preferred_element_type=jnp.float32)
    qkv_part = lax.psum_scatter(
        jnp.einsum("cre,cde->rd", grad_qkv, w_qkv, preferred_element_type=jnp.float32).astype(
            jnp.bfloat16
        ),
        "tensor",
        scatter_dimension=0,
        tiled=True,
    ).astype(jnp.float32)
    grad_inputs = lax.all_gather(
        (my_rows(grad_one) + qkv_part).astype(jnp.bfloat16), "tensor", axis=0, tiled=True
    ).astype(jnp.float32)
    grad_bqv = jnp.stack(
        [
            jnp.sum(grad_qkv[0].astype(jnp.float32), axis=0),
            jnp.sum(grad_qkv[2].astype(jnp.float32), axis=0),
        ]
    )
    grad_bup = jnp.sum(grad_pre.astype(jnp.float32), axis=0)
    grad_gain = jnp.stack([gain_one, gain_two])
    grad_shift = jnp.stack(
        [
            jnp.sum(grad_attn.astype(jnp.float32), axis=0),
            jnp.sum(grad_mlp.astype(jnp.float32), axis=0),
            shift_one,
            shift_two,
        ]
    )
    return (
        grad_inputs,
        (grad_wqkv, grad_bqv, grad_wout, grad_wup, grad_bup, grad_wdown, grad_gain, grad_shift),
    )


def deal_map(doc_ids, total_docs):
    return jnp.where(doc_ids % 2 == 1, (doc_ids + total_docs // 2) % total_docs, doc_ids)


def local_plan(seg_order, doc_lengths, seg_local, doc_local):
    total_docs = doc_lengths.shape[0]
    my_index = lax.axis_index("dp")
    doc_ids = jnp.arange(total_docs, dtype=jnp.int32)
    owner_pos = deal_map(doc_ids, total_docs)
    starts = jnp.sum((seg_order[None, :] < doc_ids[:, None]).astype(jnp.int32), axis=1)
    counts = jnp.sum((seg_order[None, :] == doc_ids[:, None]).astype(jnp.int32), axis=1)
    my_segments = my_index * seg_local + jnp.arange(seg_local, dtype=jnp.int32)
    seg_owner_doc = lax.dynamic_slice_in_dim(seg_order, my_index * seg_local, seg_local)
    seg_hot = seg_owner_doc[:, None] == doc_ids[None, :]
    my_start = jnp.sum(jnp.where(seg_hot, starts[None, :], 0), axis=1)
    my_length = jnp.sum(jnp.where(seg_hot, doc_lengths[None, :], 0), axis=1)
    my_owner = jnp.sum(jnp.where(seg_hot, owner_pos[None, :], 0), axis=1)
    within = my_segments - my_start
    valid_tokens = jnp.minimum(SEG, my_length - within * SEG)
    tok_mask = jnp.arange(SEG, dtype=jnp.int32)[None, :] < valid_tokens[:, None]
    src_slot = my_owner * MAXSEG + within
    my_deal = deal_map(my_index * doc_local + jnp.arange(doc_local, dtype=jnp.int32), total_docs)
    deal_hot = my_deal[:, None] == doc_ids[None, :]
    own_start = jnp.sum(jnp.where(deal_hot, starts[None, :], 0), axis=1)
    own_count = jnp.sum(jnp.where(deal_hot, counts[None, :], 0), axis=1)
    slot_index = jnp.arange(MAXSEG, dtype=jnp.int32)
    cross_mask = slot_index[None, :] < own_count[:, None]
    target = jnp.where(cross_mask, own_start[:, None] + slot_index[None, :], -1).reshape(-1)
    return (tok_mask, cross_mask, target, src_slot)


def picker(index_map, shard_rows):
    positions = jnp.arange(shard_rows.shape[0], dtype=jnp.int32)
    selector = (index_map[:, None] == positions[None, :]).astype(jnp.bfloat16)
    return jnp.dot(selector, shard_rows, preferred_element_type=jnp.float32)


def spreader(index_map, source_rows, row_span):
    positions = jnp.arange(row_span, dtype=jnp.int32)
    selector = (positions[:, None] == index_map[None, :]).astype(jnp.bfloat16)
    return jnp.dot(selector, source_rows, preferred_element_type=jnp.float32)


def add_terms(left, right):
    return jax.tree.map(jnp.add, left, right)


def local(
    tokens,
    seg_doc,
    doc_len,
    w_qkv,
    b_qv,
    w_out,
    w_up,
    b_up,
    w_down,
    norm_gain,
    bias_terms,
    seg_pos,
    cotangent,
):
    batches, local_rows, width = tokens.shape
    seg_local = local_rows // SEG
    doc_local = doc_len.shape[1] // lax.axis_size("dp")
    slot_rows = doc_local * MAXSEG

    def layer_weights(level):
        return (
            w_qkv[level],
            b_qv[level],
            w_out[level],
            w_up[level],
            b_up[level],
            w_down[level],
            norm_gain[level],
            bias_terms[level],
        )

    seg_weights = layer_weights(0)
    cross_weights = layer_weights(1)
    encoded = []
    grad_tokens = []
    seg_grads = []
    cross_grads = []
    pos_grads = []
    for batch_index in range(batches):
        tok_mask, cross_mask, target, src_slot = local_plan(
            seg_doc[batch_index], doc_len[batch_index], seg_local, doc_local
        )
        seg_out, seg_stored = layer_forward(
            tokens[batch_index].astype(jnp.float32), tok_mask, seg_weights
        )
        seg_cube = seg_out.reshape(seg_local, SEG, width)
        cls_rows = seg_cube[:, 0].astype(jnp.bfloat16)
        collected = picker(target, lax.all_gather(cls_rows, "dp", axis=0, tiled=True))
        cross_in = (collected.reshape(doc_local, MAXSEG, width) + seg_pos[None]).reshape(
            slot_rows, width
        )
        cross_out, cross_stored = layer_forward(cross_in, cross_mask, cross_weights)
        returned = picker(
            src_slot, lax.all_gather(cross_out.astype(jnp.bfloat16), "dp", axis=0, tiled=True)
        )
        encoded.append(
            seg_cube.at[:, 0].set(returned).reshape(local_rows, width).astype(jnp.bfloat16)
        )
        grad_cube = cotangent[batch_index].astype(jnp.float32).reshape(seg_local, SEG, width)
        grad_returned = grad_cube[:, 0].astype(jnp.bfloat16)
        grad_cross = lax.psum_scatter(
            spreader(src_slot, grad_returned, slot_rows * lax.axis_size("dp")),
            "dp",
            scatter_dimension=0,
            tiled=True,
        )
        grad_cross_in, cross_terms = layer_backward(
            grad_cross, cross_mask, cross_weights, cross_stored
        )
        pos_grads.append(jnp.sum(grad_cross_in.reshape(doc_local, MAXSEG, width), axis=0))
        grad_sent = grad_cross_in.astype(jnp.bfloat16)
        cross_grads.append(cross_terms)
        grad_cls = lax.psum_scatter(
            spreader(target, grad_sent, seg_local * lax.axis_size("dp")),
            "dp",
            scatter_dimension=0,
            tiled=True,
        )
        grad_seg = grad_cube.at[:, 0].set(grad_cls).reshape(local_rows, width)
        grad_inputs, seg_terms = layer_backward(grad_seg, tok_mask, seg_weights, seg_stored)
        grad_tokens.append(grad_inputs)
        seg_grads.append(seg_terms)
    seg_total = reduce(add_terms, seg_grads)
    cross_total = reduce(add_terms, cross_grads)
    pos_total = reduce(jnp.add, pos_grads)
    big_grads = (
        lax.psum_scatter(
            jnp.stack([seg_total[0], cross_total[0]]), "dp", scatter_dimension=2, tiled=True
        ),
        lax.psum_scatter(
            jnp.stack([seg_total[2], cross_total[2]]), "dp", scatter_dimension=2, tiled=True
        ),
        lax.psum_scatter(
            jnp.stack([seg_total[3], cross_total[3]]), "dp", scatter_dimension=1, tiled=True
        ),
        lax.psum_scatter(
            jnp.stack([seg_total[5], cross_total[5]]), "dp", scatter_dimension=2, tiled=True
        ),
    )
    small = lax.psum(
        (
            jnp.stack([seg_total[1], cross_total[1]]),
            jnp.stack([seg_total[4], cross_total[4]]),
            jnp.stack([seg_total[6], cross_total[6]]),
            jnp.stack([seg_total[7], cross_total[7]]),
            pos_total,
        ),
        "dp",
    )
    return (
        jnp.stack(encoded),
        jnp.stack(grad_tokens),
        big_grads[0],
        small[0],
        big_grads[1],
        big_grads[2],
        small[1],
        big_grads[3],
        small[2],
        small[3],
        small[4],
    )


BF = jnp.bfloat16
F32 = jnp.float32
D = 768
FF = 3072
HALF_FF = FF // 2
HALF_D = D // 2
CHUNK = 384
CHUNKS = 12
PAIRS = 6
MESH = pl.DeviceIdType.MESH
ROOT_HALF = 0.7071067811865476
PDF_SCALE = 0.3989422804014327


class Names:
    def __init__(self, **kw):
        self.__dict__.update(kw)


def mm(left, right):
    return jnp.dot(left, right, preferred_element_type=F32)


def mm_nt(left, right):
    return lax.dot_general(left, right, (((1,), (1,)), ((), ())), preferred_element_type=F32)


def span(index, size):
    return pl.ds(pl.multiple_of(index * size, size), size)


def row_norm(rows):
    centre = rows - jnp.mean(rows, axis=-1, keepdims=True)
    spread = jnp.mean(centre * centre, axis=-1, keepdims=True)
    scale = lax.rsqrt(spread + norm_eps)
    return centre * scale, scale


def stacked(pair, low_half):
    zero = jnp.zeros_like(pair)
    return jnp.concatenate(
        [jnp.where(low_half, pair, zero), jnp.where(low_half, zero, pair)], axis=0
    )


def soft_rows(scores):
    top = jnp.max(scores, axis=-1, keepdims=True)
    grown = jnp.exp(scores - top)
    return (grown * (1.0 / jnp.sum(grown, axis=-1, keepdims=True))).astype(BF)


def transpose_into(dest, source, rows):
    @pl.loop(0, rows // SEG)
    def _(s):
        dest[:, span(s, SEG)] = source[span(s, SEG), :].T


def gelu_pair(u):
    cdf = 0.5 * (1.0 + lax.erf(u * ROOT_HALF))
    slope = cdf + u * (PDF_SCALE * jnp.exp(-0.5 * u * u))
    return (u * cdf).astype(BF), slope.astype(BF)


def project(r, half):
    lanes = span(half, HALF_D)
    for c in range(3):
        r.qkv[c, :, lanes] = (mm(r.xb[...], r.wqkv[c, :, lanes]) + r.b3[c, :, lanes]).astype(BF)


def low_lanes():
    return lax.broadcasted_iota(jnp.int32, (SEG, SEG), 1) < HEAD_DIM


def attend(r, keep, first, count):
    segs = r.xb.shape[0] // SEG
    root = jnp.asarray(HEAD_DIM ** (-0.5), BF)

    @pl.loop(0, segs, unroll=min(segs, 4))
    def _(s):
        at = span(s, SEG)
        live = keep(s)
        low_half = low_lanes()
        for k in range(count):
            p = first + k
            cols = span(p, SEG)
            keys = stacked(r.qkv[1, at, cols], low_half)
            vals = stacked(r.qkv[2, at, cols], low_half)
            raw = mm_nt(r.qkv[0, at, cols] * root, keys)
            one = soft_rows(jnp.where(live, raw[:, :SEG], masked_score))
            two = soft_rows(jnp.where(live, raw[:, SEG:], masked_score))
            both = jnp.concatenate([one, two], axis=1)
            r.p[s, p] = both
            r.o[at, cols] = mm(both, vals).astype(BF)


def attn_out(r):
    for n in range(3):
        cols = slice(n * 256, n * 256 + 256)
        r.xh1[:, cols] = mm(r.o[...], r.wout[:, cols]) + r.bt[0, :, cols]


def norm_one(r, x_ref):
    rows = r.xh1.shape[0]
    block = min(rows, 256)

    @pl.loop(0, rows // block)
    def _(s):
        at = span(s, block)
        hat, scale = row_norm(x_ref[at, :].astype(F32) + r.xh1[at, :])
        r.xh1[at, :] = hat
        r.rs1[at, :] = jnp.broadcast_to(scale, (block, SEG))
        hidden = hat * r.gain[0] + r.bt[2]
        r.h1[at, :] = hidden
        r.h1b[at, :] = hidden.astype(BF)
        r.xh2[at, :] = hidden + r.bt[1]


def mlp_up(r, before):
    @pl.loop(0, 4)
    def _(j):
        before(j)
        for k in range(3):
            cols = pl.ds(pl.multiple_of(j * D + k * 256, 256), 256)
            u = mm(r.h1b[...], r.wup[:, cols]) + r.bup[:, cols]
            r.g[:, cols], r.gp[:, cols] = gelu_pair(u)


def mlp_down(r, before):
    @pl.loop(0, 2)
    def _(half):
        before(half)
        part = span(half, HALF_FF)
        for n in range(3):
            cols = slice(n * 256, n * 256 + 256)
            r.xh2[:, cols] = r.xh2[:, cols] + mm(r.g[:, part], r.wdown[part, cols])


def norm_two(r, y_ref):
    rows = r.xh2.shape[0]
    block = min(rows, 256)

    @pl.loop(0, rows // block)
    def _(s):
        at = span(s, block)
        hat, scale = row_norm(r.xh2[at, :])
        r.xh2[at, :] = hat
        r.rs2[at, :] = jnp.broadcast_to(scale, (block, SEG))
        y_ref[at, :] = (hat * r.gain[1] + r.bt[3]).astype(BF)


def norm_back(grad, hat, scale, gain):
    d_hat = grad * gain
    first = jnp.mean(d_hat, axis=-1, keepdims=True)
    second = jnp.mean(d_hat * hat, axis=-1, keepdims=True)
    return (d_hat - first - hat * second) * scale


def norm_back_rows(r, hat_ref, scale_ref, gain, grad_of):
    zero = jnp.zeros((1, D), F32)
    rows = r.dr.shape[0]
    block = min(rows, 256)

    def step(s, sums):
        at = span(s, block)
        grad = grad_of(s, at)
        hat = hat_ref[at, :]
        out = norm_back(grad, hat, scale_ref[at, 0:1], gain)
        low = out.astype(BF)
        r.dr[at, :] = out
        r.dm[at, :] = low
        return (
            sums[0] + jnp.sum(grad * hat, axis=0, keepdims=True),
            sums[1] + jnp.sum(grad, axis=0, keepdims=True),
            sums[2] + jnp.sum(low.astype(F32), axis=0, keepdims=True),
        )

    sums = lax.fori_loop(0, rows // block, step, (zero, zero, zero))
    transpose_into(r.dmt, r.dm, rows)
    return sums


def back_norm_two(r, grad_of):
    sums = norm_back_rows(r, r.xh2, r.rs2, r.gain[1], grad_of)
    r.small_common[1], r.small_common[5], r.small_common[3] = sums


def back_norm_one(r):
    sums = norm_back_rows(r, r.xh1, r.rs1, r.gain[0], lambda s, at: r.dr[at, :])
    r.small_common[0], r.small_common[4], r.small_common[2] = sums


def grad_hidden(r):
    @pl.loop(0, 3)
    def _(j):
        cols = span(j, 1024)
        du = (mm_nt(r.dm[...], r.wdown[cols, :]) * r.gp[:, cols].astype(F32)).astype(BF)
        r.gp[:, cols] = du
        r.bup_sum[:, cols] = jnp.sum(du.astype(F32), axis=0, keepdims=True)


def grad_middle(r):
    @pl.loop(0, 2)
    def _(n):
        cols = span(n, CHUNK)
        r.dr[:, cols] = r.dr[:, cols] + mm_nt(r.gp[...], r.wup[cols, :])


def grad_heads(r):
    for n in range(3):
        cols = slice(n * 256, n * 256 + 256)
        r.dh[:, cols] = mm_nt(r.dm[...], r.wout[cols, :]).astype(BF)


def attend_back_values(r):
    segs = r.dh.shape[0] // SEG

    @pl.loop(0, segs, unroll=min(segs, 2))
    def _(s):
        at = span(s, SEG)
        low_half = low_lanes()
        for p in range(PAIRS):
            d_vals = mm(r.p[s, p].T, r.dh[at, p * SEG : p * SEG + SEG])
            cols = slice(2 * D + p * SEG, 2 * D + p * SEG + SEG)
            r.g[at, cols] = jnp.where(low_half, d_vals[:SEG], d_vals[SEG:]).astype(BF)


def attend_back(r, exact, before):
    root = jnp.asarray(HEAD_DIM ** (-0.5), BF)
    segs = r.dh.shape[0] // SEG
    together = min(segs, 2)

    def segment(s):
        at = span(s, SEG)
        low_half = low_lanes()
        head = lax.broadcasted_iota(jnp.int32, (SEG, 2 * SEG), 0) < HEAD_DIM
        side = lax.broadcasted_iota(jnp.int32, (SEG, 2 * SEG), 1) < SEG
        ones = jnp.where(head == side, 1.0, 0.0).astype(BF)
        for p in range(PAIRS):
            cols = slice(p * SEG, p * SEG + SEG)
            query = r.qkv[0, at, cols] * root
            keys = stacked(r.qkv[1, at, cols] * root, low_half)
            vals = stacked(r.qkv[2, at, cols], low_half)
            d_head = r.dh[at, cols]
            d_probs = mm_nt(d_head, vals)
            both = d_head.astype(F32) * r.o[at, cols].astype(F32)
            inner = mm(both.astype(BF), ones)
            if exact:
                inner = inner + mm((both - both.astype(BF).astype(F32)).astype(BF), ones)
            d_scores = (r.p[s, p].astype(F32) * (d_probs - inner)).astype(BF)
            d_keys = mm(d_scores.T, query)
            r.g[at, cols] = mm(d_scores, keys).astype(BF)
            cols = slice(D + p * SEG, D + p * SEG + SEG)
            r.g[at, cols] = jnp.where(low_half, d_keys[:SEG], d_keys[SEG:]).astype(BF)

    @pl.loop(0, segs // together)
    def _(i):
        before(i)
        for k in range(together):
            segment(i * together + k)


def bias_heads(r):
    for c in (0, 2):
        r.qv_sum[c // 2] = jnp.sum(
            r.g[:, c * D : (c + 1) * D].astype(F32), axis=0, keepdims=True
        )


def grad_input(r):
    for n in range(3):
        cols = slice(n * 256, n * 256 + 256)
        total = r.dr[:, cols]
        for c in range(3):
            total = total + mm_nt(r.g[:, c * D : (c + 1) * D], r.wqkv[c, cols, :])
        r.dr[:, cols] = total


def chunk_operands(r, c):
    if c < 4:
        return r.dmt, (r.g, c * CHUNK, HALF_FF + c * CHUNK)
    if c < 8:
        return r.h1t, (r.gp, (c - 4) * CHUNK, HALF_FF + (c - 4) * CHUNK)
    if c == 8:
        return r.dmt, (r.o, 0, HALF_D)
    at = QKV_OF[c - 9] * D
    return r.xt, (r.g, at, at + HALF_D)


QKV_OF = (2, 0, 1)
HOOK_CHUNKS = {"down": (0, 4), "up": (4, 8), "out": (8, 9), "qkv": (9, 12), "v": (9, 10), "qk": (10, 12)}


class Copies:
    def __init__(self, sems):
        self.sems = sems
        self.used = 0

    def start(self, source, dest):
        copy = pltpu.make_async_copy(source, dest, self.sems.at[self.used])
        self.used += 1
        copy.start()
        return copy


def remote(source, dest, send_sem, recv_sem, device):
    return pltpu.make_async_remote_copy(
        src_ref=source,
        dst_ref=dest,
        send_sem=send_sem,
        recv_sem=recv_sem,
        device_id=device,
        device_id_type=MESH,
    )


class Gather:
    def __init__(self, dp, everyone, send, recv):
        self.dp, self.everyone, self.send, self.recv = dp, everyone, send, recv

    def start(self, block):
        d, t = lax.axis_index("dp"), lax.axis_index("tensor")
        everyone = self.everyone
        everyone[d] = block
        for o in range(1, self.dp):
            peer = (lax.rem(d + o, self.dp), t)
            copy = remote(everyone.at[d], everyone.at[d], self.send.at[o], self.recv.at[d], peer)
            copy.start()

    def sent(self):
        d, t = lax.axis_index("dp"), lax.axis_index("tensor")
        block = self.everyone.at[d]
        for o in range(1, self.dp):
            peer = (lax.rem(d + o, self.dp), t)
            remote(block, block, self.send.at[o], self.recv.at[d], peer).wait_send()

    def arrived(self):
        d, t = lax.axis_index("dp"), lax.axis_index("tensor")
        for o in range(1, self.dp):
            source = lax.rem(d + o, self.dp)
            block = self.everyone.at[source]
            remote(block, block, self.send.at[o], self.recv.at[source], (source, t)).wait_recv()

    def rows_into(self, dest):
        segs = self.everyone.shape[1]
        pack = 8 // segs
        for i in range(self.dp // pack):
            blocks = [self.everyone[i * pack + k].astype(F32) for k in range(pack)]
            dest[i * 8 : i * 8 + 8, :] = jnp.concatenate(blocks, axis=0)


SLOTS = 4
RING = 9
WEIGHTS = ("wqkv", "wout", "wup", "wdown")


def half_of(ref, which, half):
    if which == "wqkv":
        return ref.at[:, :, half * HALF_D : (half + 1) * HALF_D]
    if which == "wout":
        return ref.at[half * HALF_D : (half + 1) * HALF_D, :]
    if which == "wup_square":
        return ref.at[:, half * HALF_D : (half + 1) * HALF_D]
    if which == "wup":
        return ref.at[:, half * HALF_FF : (half + 1) * HALF_FF]
    return ref.at[half * HALF_FF : (half + 1) * HALF_FF, :]


def fill_bias(b3, bup, half, layer, b_qv, b_up):
    lanes = slice(half * HALF_D, (half + 1) * HALF_D)
    b3[0, :, lanes] = b_qv[layer, 0:1, :]
    b3[1, :, lanes] = jnp.zeros((1, HALF_D), F32)
    b3[2, :, lanes] = b_qv[layer, 1:2, :]
    bup[:, half * HALF_FF : (half + 1) * HALF_FF] = b_up[layer : layer + 1, :]


def pack_halves(r):
    for half in range(2):
        at = 6 + 3 * half
        lanes = slice(half * HALF_D, (half + 1) * HALF_D)
        r.small[at, :, 0:HALF_D] = r.qv_sum[0, :, lanes]
        r.small[at, :, HALF_D:] = r.qv_sum[1, :, lanes]
        base = half * HALF_FF
        r.small[at + 1] = r.bup_sum[:, base : base + D]
        r.small[at + 2] = r.bup_sum[:, base + D : base + 2 * D]


def first_of_segments(ref, segs):
    return jnp.concatenate(
        [ref[s * SEG : s * SEG + 16, :].astype(F32)[0:1] for s in range(segs)], axis=0
    )


class Stream:
    ORDER = (
        [("qkv", c) for c in range(3)] + [("out", 0)] + [("up", j) for j in range(4)]
        + [("down", j) for j in range(4)] * 2
        + [("up", j) for j in range(4)] + [("out", 0)] + [("qkv", c) for c in range(3)]
    )
    DEPTH = 4

    def __init__(self, r, arriving):
        self.r = r
        self.arriving = arriving
        self.next = 0
        self.pending = []

    def copies(self, n):
        r = self.r
        kind, index = self.ORDER[n]
        which = "w" + kind
        halves = (getattr(r, "a_" + which).at[1], getattr(r, "f_" + which))
        dest, sems = r.ring_w.at[n % self.DEPTH], r.ring_sem.at[n % self.DEPTH]
        if kind == "qkv":
            pairs = [(halves[h].at[index], half_of(dest, "wup_square", h)) for h in range(2)]
        elif kind == "out":
            pairs = [(halves[h], half_of(dest, "wout", h)) for h in range(2)]
        else:
            at = slice(index % 2 * D, index % 2 * D + D)
            source = halves[index // 2]
            pairs = [(source.at[:, at] if kind == "up" else source.at[at, :], dest)]
        return [pltpu.make_async_copy(a, b, sems.at[k]) for k, (a, b) in enumerate(pairs)]

    def start(self, n):
        if n < len(self.ORDER):
            kind, index = self.ORDER[n]
            if index >= 2 and kind in self.arriving:
                self.arriving.pop(kind).wait_recv()
            self.pending.append(self.copies(n))
            for copy in self.pending[-1]:
                copy.start()

    def take(self, body):
        for copy in self.pending.pop(0):
            copy.wait()
        kind, index = self.ORDER[self.next]
        body(index, self.r.ring_w.at[self.next % self.DEPTH])
        self.start(self.next + self.DEPTH)
        self.next += 1


def cross_layer(r, q, stream, keep, pump, hooks):
    def lanes(j):
        return slice(j * D, (j + 1) * D)

    def project_piece(c, w):
        q.qkv[c] = (mm(q.xb[...], w[...]) + q.b3[c]).astype(BF)

    for c in range(3):
        stream.take(project_piece)
    attend(q, keep, 0, PAIRS)
    pump("attend")

    def out_piece(j, w):
        q.xh1[...] = mm(q.o[...], w[...]) + q.bt[0]

    stream.take(out_piece)
    norm_one(q, q.x32)
    transpose_into(q.h1t, q.h1b, SEG)

    def up_piece(j, w):
        u = mm(q.h1b[...], w[...]) + q.bup[:, lanes(j)]
        q.g[:, lanes(j)], q.gp[:, lanes(j)] = gelu_pair(u)

    for j in range(4):
        stream.take(up_piece)
    pump("up")

    def down_piece(j, w):
        q.xh2[...] = q.xh2[...] + mm(q.g[:, lanes(j)], w[...])

    for j in range(4):
        stream.take(down_piece)
    norm_two(q, q.yb)
    pump("down")
    back_norm_two(q, lambda s, at: q.dy[at, :])
    hooks("down")

    def back_down_piece(j, w):
        du = (mm_nt(q.dm[...], w[...]) * q.gp[:, lanes(j)].astype(F32)).astype(BF)
        q.gp[:, lanes(j)] = du
        r.bup_sum[:, lanes(j)] = jnp.sum(du.astype(F32), axis=0, keepdims=True)

    for j in range(4):
        stream.take(back_down_piece)
    pump("back_down")
    hooks("up")

    def back_up_piece(j, w):
        q.dr[...] = q.dr[...] + mm_nt(q.gp[:, lanes(j)], w[...])

    for j in range(4):
        stream.take(back_up_piece)
    pump("back_up")
    back_norm_one(q)
    hooks("out")

    def back_out_piece(j, w):
        q.dh[...] = mm_nt(q.dm[...], w[...]).astype(BF)

    stream.take(back_out_piece)
    attend_back_values(q)
    attend_back(q, True, lambda i: None)
    bias_heads(q)
    pump("attend_back")
    hooks("qkv")

    def back_qkv_piece(c, w):
        q.dr[...] = q.dr[...] + mm_nt(q.g[:, lanes(c)], w[...])

    for c in range(3):
        stream.take(back_qkv_piece)


def whole_kernel(dp, names, *refs):
    r = Names(**dict(zip(names, refs)))
    d, t = lax.axis_index("dp"), lax.axis_index("tensor")
    x, y, z = lax.rem(d, 2), lax.rem(lax.div(d, 2), 2), lax.div(d, 4)
    zs = dp // 4
    shard = D // dp
    rows = r.xb.shape[0]
    segs = rows // SEG
    sibling = (d, 1 - t)
    x_peer = (z * 4 + y * 2 + (1 - x), t)
    y_peer = (z * 4 + (1 - y) * 2 + x, t)
    z_peers = [(lax.rem(z + o, zs) * 4 + y * 2 + x, t) for o in range(1, zs)]
    r.dr, r.dm, r.y1, r.dh = r.h1, r.h1b, r.xb, r.cot

    barrier = pltpu.get_barrier_semaphore()
    for device in [sibling] + [(lax.rem(d + o, dp), t) for o in range(1, dp)]:
        pl.semaphore_signal(barrier, inc=1, device_id=device, device_id_type=MESH)
    copies = Copies(r.local_sem)
    for layer, gain, terms in ((0, r.gain, r.bt), (1, r.gain_cross, r.bt_cross)):
        for k in range(2):
            gain[k] = r.norm_gain[layer, k : k + 1, :]
        for k in range(4):
            terms[k] = r.bias_terms[layer, k : k + 1, :]
    own = {w: getattr(r, "a_" + w) for w in WEIGHTS}
    full = {w: getattr(r, "f_" + w) for w in WEIGHTS}
    load_x = copies.start(r.tokens.at[t], r.xb)
    loads = {w: copies.start(own[w].at[0], half_of(getattr(r, w), w, 0)) for w in WEIGHTS}
    load_cot = copies.start(r.cotangent.at[t], r.cot)
    load_x.wait()
    transpose_into(r.xt, r.xb, rows)
    fill_bias(r.b3, r.bup, 0, 0, r.b_qv, r.b_up)
    fill_bias(r.b3_cross, r.bup_cross, 0, 1, r.b_qv, r.b_up)
    swaps = {}

    def described(layer, w):
        k = WEIGHTS.index(w)
        dest = half_of(getattr(r, w), w, 1) if layer == 0 else full[w]
        return remote(own[w].at[layer], dest, r.w_send.at[layer, k], r.w_recv.at[layer, k], sibling)

    for layer in range(2):
        for w in WEIGHTS:
            swaps[layer, w] = described(layer, w)

    def swap(layer, w):
        swaps[layer, w].start()

    cot_gather = Gather(dp, r.cot_all, r.g_send.at[0], r.g_recv.at[0])
    cls_gather = Gather(dp, r.cls_all, r.g_send.at[1], r.g_recv.at[1])
    hat_gather = Gather(dp, r.hat_all, r.g_send.at[2], r.g_recv.at[2])
    act_gather = Gather(dp, r.act_all, r.g_send.at[3], r.g_recv.at[3])

    def keep(s):
        seg = d * segs + s
        doc = r.seg_doc[t, seg]
        within = jnp.int32(0)
        for back in range(1, MAXSEG):
            same = r.seg_doc[t, jnp.maximum(seg - back, 0)] == doc
            within = within + jnp.where(jnp.logical_and(seg >= back, same), 1, 0)
        valid = jnp.minimum(SEG, r.doc_len[t, doc] - SEG * within)
        return lax.broadcasted_iota(jnp.int32, (1, SEG), 1) < valid

    def start_swaps():
        pl.semaphore_wait(barrier, dp)
        swap(0, "wqkv")
        for copy in swap_bias:
            copy.start()
        swap(0, "wout")
        swap(0, "wup")
        load_cot.wait()
        cot_gather.start(first_of_segments(r.cot, segs).astype(BF))

    def take_other():
        for copy in swap_bias:
            copy.wait_recv()
        fill_bias(r.b3, r.bup, 1, 0, r.x_bqv, r.x_bup)
        fill_bias(r.b3_cross, r.bup_cross, 1, 1, r.x_bqv, r.x_bup)
        swaps[0, "wqkv"].wait_recv()

    swap_bias = [
        remote(r.b_qv, r.x_bqv, r.w_send.at[0, 4], r.w_recv.at[0, 4], sibling),
        remote(r.b_up, r.x_bup, r.w_send.at[1, 4], r.w_recv.at[1, 4], sibling),
    ]
    loads["wqkv"].wait()

    @pl.loop(0, 2)
    def _(half):
        pl.when(half == 1)(take_other)
        project(r, half)
        pl.when(half == 0)(start_swaps)
        attend(r, keep, half * (PAIRS // 2), PAIRS // 2)

    swap(0, "wdown")
    loads["wout"].wait()
    swaps[0, "wout"].wait_recv()
    attn_out(r)
    norm_one(r, r.xb)
    loads["wup"].wait()
    mlp_up(r, lambda j: pl.when(j == 2)(swaps[0, "wup"].wait_recv))
    transpose_into(r.h1t, r.h1b, rows)
    loads["wdown"].wait()
    mlp_down(r, lambda half: pl.when(half == 1)(swaps[0, "wdown"].wait_recv))
    swap(1, "wqkv")
    swap(1, "wout")
    norm_two(r, r.y1)
    cls_gather.start(first_of_segments(r.y1, segs).astype(BF))
    hats = first_of_segments(r.xh2, segs)
    hat_gather.start(jnp.concatenate([hats, first_of_segments(r.rs2, segs)], axis=1))

    def sib_copy(c):
        slot = lax.rem(c, SLOTS)
        return remote(
            r.sib_out.at[slot], r.sib_in.at[slot], r.sib_send.at[slot], r.sib_recv.at[slot], sibling
        )

    def ring(c):
        return lax.rem(c, RING)

    low_z, high_z = slice(0, zs // 2), slice(zs // 2, zs)

    def stage_one(c):
        g, into = r.gbuf.at[ring(c)], r.one_in.at[ring(c)]
        return (
            remote(g.at[low_z, :, 1 - x], into.at[0], r.one_send.at[c, 0], r.one_recv.at[c, 0], x_peer),
            remote(g.at[high_z, 1 - y], into.at[1], r.one_send.at[c, 1], r.one_recv.at[c, 1], y_peer),
        )

    def stage_two(c):
        g, into = r.gbuf.at[ring(c)], r.two_in.at[ring(c)]
        return (
            remote(g.at[low_z, 1 - y, x], into.at[0], r.two_send.at[c, 0], r.two_recv.at[c, 0], y_peer),
            remote(g.at[high_z, y, 1 - x], into.at[1], r.two_send.at[c, 1], r.two_recv.at[c, 1], x_peer),
        )

    def stage_three(c):
        g, into = r.gbuf.at[ring(c)], r.three_in.at[ring(c)]
        return [
            remote(
                g.at[lax.rem(z + o, zs), y, x],
                into.at[o - 1],
                r.three_send.at[c, o - 1],
                r.three_recv.at[c, o - 1],
                z_peers[o - 1],
            )
            for o in range(1, zs)
        ]

    def emit_other(c, left, right, at):
        @pl.when(c >= SLOTS)
        def _():
            sib_copy(c).wait_send()
            pl.semaphore_wait(r.credit, 1)

        r.sib_out[lax.rem(c, SLOTS)] = mm(left[...], right[:, pl.ds(at, CHUNK)]).astype(BF)
        sib_copy(c).start()

    def emit_own(c, left, right, at):
        mine = mm(left[...], right[:, pl.ds(at, CHUNK)])
        sib_copy(c).wait_recv()
        mine = (mine + r.sib_in[lax.rem(c, SLOTS)].astype(F32)).astype(BF)
        r.gbuf[ring(c)] = mine.reshape(zs, 2, 2, shard, CHUNK)

        @pl.when(c < CHUNKS - SLOTS)
        def _():
            pl.semaphore_signal(r.credit, inc=1, device_id=sibling, device_id_type=MESH)

    def launch(*chunks):
        for c in chunks:
            for copy in stage_one(jnp.int32(c)):
                copy.start()

    def hooks(name, which, part=None):
        low, high = HOOK_CHUNKS[name]
        left, (right, own_at, other_at) = chunk_operands(r, low)
        step = D if name == "qk" else CHUNK

        def at(c, base):
            return pl.multiple_of((c - low) * step + base, SEG)

        if which == "other":

            @pl.loop(low, high)
            def _(c):
                emit_other(c, left, right, at(c, other_at))

        else:

            @pl.loop(*(part or (low, high)))
            def _(c):
                emit_own(c, left, right, at(c, own_at))
                if which == "launch":
                    for copy in stage_one(c):
                        copy.start()

    def second(*chunks):
        for c in chunks:
            c = jnp.int32(c)
            g, into = r.gbuf.at[ring(c)], r.one_in.at[ring(c)]
            from_x, from_y = stage_one(c)
            to_y, to_x = stage_two(c)
            from_x.wait_recv()
            g[low_z, :, x] = g[low_z, :, x] + into[0]
            to_y.start()
            from_y.wait_recv()
            g[high_z, y] = g[high_z, y] + into[1]
            to_x.start()

    def third(*chunks):
        for c in chunks:
            c = jnp.int32(c)
            g, into = r.gbuf.at[ring(c)], r.two_in.at[ring(c)]
            for copy in stage_two(c):
                copy.wait_recv()
            g[low_z, y, x] = g[low_z, y, x] + into[0]
            g[high_z, y, x] = g[high_z, y, x] + into[1]
            for copy in stage_three(c):
                copy.start()

    def finish(*chunks):
        for c in chunks:
            at = jnp.int32(c)
            total = r.gbuf[ring(at), z, y, x].astype(F32)
            for o, copy in enumerate(stage_three(at)):
                copy.wait_recv()
                total = total + r.three_in[ring(at), o].astype(F32)
            r.mine[c] = r.mine[c] + total if c < 4 else total
            for copy in (*stage_one(at), *stage_two(at), *stage_three(at)):
                copy.wait_send()

    block_row = lax.broadcasted_iota(jnp.int32, (256, 1), 0)

    def without_first(s, at):
        return jnp.where(lax.rem(block_row, SEG) == 0, 0.0, r.cot[at, :].astype(F32))

    r.act_first[...] = first_of_segments(r.g, segs)
    r.small_common = r.small
    back_norm_two(r, without_first)
    hooks("down", "other")
    swap(1, "wup")
    hooks("down", "launch")
    swap(1, "wdown")
    act_gather.start(r.act_first[...].astype(BF))

    q = Names(
        **{k: getattr(r, "q_" + k) for k in CROSS},
        g=r.g.at[0:SEG],
        gp=r.g.at[SEG : 2 * SEG],
        gain=r.gain_cross,
        bt=r.bt_cross,
        b3=r.b3_cross,
        bup=r.bup_cross,
        qv_sum=r.qv_sum,
    )
    q.dr, q.dm, q.small_common = q.h1, q.h1b, r.small1
    slots = q.xb.shape[0]
    total_docs = slots // MAXSEG
    total_segs = dp * segs
    stream = Stream(r, {"up": swaps[1, "wup"], "down": swaps[1, "wdown"]})
    for w in ("wqkv", "wout"):
        swaps[1, w].wait_recv()
    for n in range(stream.DEPTH):
        stream.start(n)

    doc = jnp.where(t == 0, r.seg_doc_v[0:1, :], r.seg_doc_v[1:2, :])
    below = lax.broadcasted_iota(jnp.int32, (total_segs, total_segs), 0)
    across = lax.broadcasted_iota(jnp.int32, (total_segs, total_segs), 1)

    def column(row):
        wide = jnp.broadcast_to(row, (total_segs, total_segs))
        return jnp.sum(jnp.where(below == across, wide, 0.0), axis=1, keepdims=True)

    doc_f = doc.astype(F32)
    earlier = jnp.logical_and(column(doc_f) == doc_f, below < across)
    within = jnp.sum(jnp.where(earlier, 1.0, 0.0), axis=0, keepdims=True).astype(jnp.int32)
    moved = doc + total_docs // 2
    moved = jnp.where(moved >= total_docs, moved - total_docs, moved)
    slot_of = (jnp.where((doc & 1) == 1, moved, doc) * MAXSEG + within).astype(F32)
    slot_ids = lax.broadcasted_iota(jnp.int32, (slots, total_segs), 0).astype(F32)
    deal = jnp.where(slot_ids == slot_of, 1.0, 0.0).astype(BF)
    slot_row = lax.broadcasted_iota(jnp.int32, (total_segs, slots), 1).astype(F32)
    r.undeal[...] = jnp.where(slot_row == column(slot_of), 1.0, 0.0).astype(BF)
    pick_row = lax.broadcasted_iota(jnp.int32, (8, total_segs), 0)
    pick_seg = lax.broadcasted_iota(jnp.int32, (8, total_segs), 1)
    picked = jnp.logical_and(pick_row < segs, pick_seg == d * segs + pick_row)
    r.back[...] = mm(jnp.where(picked, 1.0, 0.0).astype(BF), r.undeal[...]).astype(BF)
    live = mm_nt(jnp.ones((8, total_segs), BF), deal)[0:1] > 0.5
    key_doc = lax.broadcasted_iota(jnp.int32, (SEG, SEG), 1) >> 3
    row_doc = lax.broadcasted_iota(jnp.int32, (SEG, SEG), 0) >> 3
    r.allowed[...] = jnp.where(jnp.logical_and(key_doc == row_doc, live), 1.0, 0.0)

    cot_gather.arrived()
    cot_gather.rows_into(r.rows64)
    q.dy[...] = mm(deal, r.rows64[...].astype(BF))
    cls_gather.arrived()
    cls_gather.rows_into(r.rows64)
    q.x32[...] = mm(deal, r.rows64[...].astype(BF)) + jnp.concatenate(
        [r.seg_pos[...]] * total_docs, axis=0
    )
    q.xb[...] = q.x32[...].astype(BF)
    transpose_into(q.xt, q.xb, slots)

    def cross_hooks(name):
        low, high = HOOK_CHUNKS[name]
        for c in range(low, high):
            left, (right, own_at, other_at) = chunk_operands(q, c)
            mine = left[pl.ds(pl.multiple_of(d * shard, 16), shard), :]
            r.shard1[c] = mm(mine, right[:, own_at : own_at + CHUNK])
            r.shard_out[c] = mm(mine, right[:, other_at : other_at + CHUNK]).astype(BF)

    def pump(point):
        if point == "back_up":
            second(0, 1)
        elif point == "attend_back":
            second(2, 3)

    cross_layer(r, q, stream, lambda s: r.allowed[...] > 0.5, pump, cross_hooks)
    r.small, keep_small = r.small1, r.small
    pack_halves(r)
    r.small = keep_small
    total = q.dr[0:MAXSEG, :]
    for j in range(1, total_docs):
        total = total + q.dr[j * MAXSEG : (j + 1) * MAXSEG, :]
    for k in range(MAXSEG):
        r.small1[12 + k] = total[k : k + 1, :]
    r.ret[...] = mm(r.back[...], q.yb[...])
    low = q.dr[...].astype(BF)
    r.dc[...] = mm(r.back[...], low)

    gain_sum = jnp.zeros((1, D), F32)
    shift_sum, low_sum = gain_sum, gain_sum
    top = lax.broadcasted_iota(jnp.int32, (16, 1), 0) == 0
    for s in range(segs):
        at = slice(s * SEG, s * SEG + 16)
        grad = jnp.where(top, r.dc[s : s + 1, :], 0.0)
        hat = r.xh2[at, :]
        out = jnp.where(top, norm_back(grad, hat, r.rs2[at, 0:1], r.gain[1]), 0.0)
        out_low = out.astype(BF)
        r.dr[at, :] = jnp.where(top, out, r.dr[at, :])
        r.dm[at, :] = jnp.where(top, out_low.astype(F32), r.dm[at, :].astype(F32)).astype(BF)
        gain_sum = gain_sum + jnp.sum(grad * hat, axis=0, keepdims=True)
        shift_sum = shift_sum + jnp.sum(grad, axis=0, keepdims=True)
        low_sum = low_sum + jnp.sum(out_low.astype(F32), axis=0, keepdims=True)
        r.y1[at, :] = jnp.where(top, r.ret[s : s + 1, :], r.y1[at, :].astype(F32)).astype(BF)
    r.small_common[1] = r.small_common[1] + gain_sum
    r.small_common[5] = r.small_common[5] + shift_sum
    r.small_common[3] = r.small_common[3] + low_sum
    outs = [copies.start(r.y1, r.o_enc.at[t])]
    enc_swap = remote(r.y1, r.o_enc.at[t], r.misc_send.at[0], r.misc_recv.at[0], sibling)
    enc_swap.start()

    hat_gather.arrived()
    hat_gather.rows_into(r.hat64)
    act_gather.arrived()
    act_gather.rows_into(r.act64)
    all_grads = mm(r.undeal[...], low)
    late = norm_back(all_grads, r.hat64[:, 0:D], r.hat64[:, D : D + 1], r.gain[1]).astype(BF)
    r.late[0:total_segs, :] = late
    r.late[total_segs:, :] = jnp.zeros((SEG - total_segs, D), BF)
    transpose_into(r.late_t, r.late, SEG)
    mine = r.late_t[pl.ds(pl.multiple_of(d * shard, 16), shard), 0:total_segs]
    for c in range(4):
        for half in range(2):
            cols = slice(half * HALF_FF + c * CHUNK, half * HALF_FF + (c + 1) * CHUNK)
            part = mm(mine, r.act64[:, cols].astype(BF))
            if half == 0:
                r.mine[c] = part
            else:
                r.shard_out[CHUNKS + c] = part.astype(BF)
    cross_swap = [
        remote(r.shard_out, r.shard_in, r.misc_send.at[1], r.misc_recv.at[1], sibling),
        remote(r.small1.at[0:6], r.small1_in.at[0:6], r.misc_send.at[2], r.misc_recv.at[2], sibling),
        remote(r.small1.at[9:20], r.small1_in.at[6:17], r.misc_send.at[3], r.misc_recv.at[3], sibling),
    ]
    for copy in cross_swap:
        copy.start()

    third(0, 1)
    grad_hidden(r)
    third(2, 3)
    hooks("up", "other")
    hooks("up", "own")
    launch(4, 5)
    grad_middle(r)
    for copy in cross_swap:
        copy.wait()
    for c in range(CHUNKS):
        r.shard1[c] = r.shard1[c] + r.shard_in[c].astype(F32)
    r.o_small[9:26] = (
        jnp.concatenate([r.small1[0:9], r.small1[12:20]], axis=0) + r.small1_in[...]
    )
    outs.append(copies.start(r.shard1, r.o_shard.at[1]))
    back_norm_one(r)
    second(4)
    launch(6)
    hooks("out", "other")
    grad_heads(r)
    hooks("out", "own")
    second(5)
    launch(7)
    attend_back_values(r)
    hooks("v", "other")
    finish(0, 1, 2, 3)
    for c in range(4):
        r.mine[c] = r.mine[c] + r.shard_in[CHUNKS + c].astype(F32)

    def halfway():
        second(6)
        third(4)
        hooks("v", "own")
        launch(8, 9)

    attend_back(r, False, lambda i: pl.when(i == 1)(halfway))
    bias_heads(r)
    pack_halves(r)
    small_swap = [
        remote(r.small.at[0:6], r.small_in.at[0:6], r.misc_send.at[4], r.misc_recv.at[4], sibling),
        remote(r.small.at[9:12], r.small_in.at[6:9], r.misc_send.at[5], r.misc_recv.at[5], sibling),
    ]
    for copy in small_swap:
        copy.start()
    hooks("qk", "other")
    second(7)
    third(5)
    for copy in small_swap:
        copy.wait()
    r.total[...] = r.small[0:9] + r.small_in[...]
    x_small = remote(r.total, r.x_small, r.misc_send.at[7], r.misc_recv.at[7], x_peer)
    x_small.start()
    hooks("qk", "own")
    launch(10, 11)
    x_small.wait()
    r.total_x[...] = r.total[...] + r.x_small[...]
    y_small = remote(r.total_x, r.y_small, r.misc_send.at[8], r.misc_recv.at[8], y_peer)
    y_small.start()
    third(6)
    second(8)
    grad_input(r)
    grad_swap = remote(r.dr, r.o_grad.at[t], r.misc_send.at[6], r.misc_recv.at[6], sibling)
    grad_swap.start()
    outs.append(copies.start(r.dr, r.o_grad.at[t]))
    third(7)
    y_small.wait()
    r.z_small[z] = r.total_x[...] + r.y_small[...]
    z_sends = []
    for o in range(1, zs):
        z_sends.append(
            remote(r.z_small.at[z], r.z_small.at[z], r.z_send.at[o], r.z_recv.at[z], z_peers[o - 1])
        )
        z_sends[-1].start()
    second(9)
    finish(4)
    third(8)
    second(10)
    finish(5)
    third(9)
    second(11)
    finish(6, 7)
    third(10)
    for o in range(1, zs):
        source = lax.rem(z + o, zs)
        block = r.z_small.at[source]
        remote(block, block, r.z_send.at[o], r.z_recv.at[source], z_peers[o - 1]).wait_recv()
    total = r.z_small[0]
    for k in range(1, zs):
        total = total + r.z_small[k]
    r.o_small[0:9] = total
    third(11)
    finish(8, 9, 10, 11)
    outs.append(copies.start(r.mine, r.o_shard.at[0]))

    for copy in z_sends:
        copy.wait_send()
    for c in range(CHUNKS - SLOTS, CHUNKS):
        sib_copy(jnp.int32(c)).wait_send()
    for gathered in (cot_gather, cls_gather, hat_gather, act_gather):
        gathered.sent()
    for copy in swap_bias:
        copy.wait_send()
    for copy in swaps.values():
        copy.wait_send()
    grad_swap.wait()
    enc_swap.wait()
    for copy in outs:
        copy.wait()


CROSS = ("xb", "x32", "xt", "h1t", "h1b", "h1", "qkv", "o", "p", "xh1", "rs1", "xh2", "rs2", "yb", "dy", "dmt", "dh")
WEIGHT_SCRATCH = dict(
    wqkv=((3, D, D), BF), wout=((D, D), BF), wup=((D, FF), BF), wdown=((FF, D), BF)
)
BACK_SCRATCH = dict(qv_sum=((2, 1, D), F32), bup_sum=((1, FF), F32))


def saved_shapes(rows):
    return dict(
        xt=((D, rows), BF),
        h1t=((D, rows), BF),
        qkv=((3, rows, D), BF),
        o=((rows, D), BF),
        p=((rows // SEG, PAIRS, SEG, 2 * SEG), BF),
        xh1=((rows, D), F32),
        rs1=((rows, SEG), F32),
        g=((rows, FF), BF),
        gp=((rows, FF), BF),
        xh2=((rows, D), F32),
        rs2=((rows, SEG), F32),
    )


def forward_shapes(rows):
    return dict(
        xb=((rows, D), BF),
        h1=((rows, D), F32),
        h1b=((rows, D), BF),
        b3=((3, 1, D), F32),
        bup=((1, FF), F32),
    )


def vmem(table):
    return [pltpu.VMEM(shape, kind) for shape, kind in table.values()]


def arrays(table):
    return [jax.ShapeDtypeStruct(shape, kind) for shape, kind in table.values()]


def run_whole(dp, inputs):
    hbm = pl.BlockSpec(memory_space=pl.ANY)
    small = pl.BlockSpec(memory_space=pltpu.VMEM)
    smem = pl.BlockSpec(memory_space=pltpu.SMEM)
    batches, rows, _ = inputs["tokens"].shape
    slots = inputs["doc_len"].shape[1] * MAXSEG
    segs = rows // SEG
    total_segs = dp * segs
    zs = dp // 4
    shard = D // dp
    outs = dict(
        o_enc=((batches, rows, D), BF),
        o_grad=((batches, rows, D), F32),
        o_shard=((2, CHUNKS, shard, CHUNK), F32),
        o_small=((26, 1, D), F32),
    )
    outs.update({"f_" + w: (inputs["a_" + w].shape[1:], BF) for w in WEIGHTS})
    scratch = dict(saved_shapes(rows))
    scratch.update(WEIGHT_SCRATCH)
    scratch.update(forward_shapes(rows))
    scratch.update(BACK_SCRATCH)
    cross = dict(saved_shapes(slots))
    cross.update(forward_shapes(slots))
    cross.update(
        x32=((slots, D), F32), yb=((slots, D), BF), dy=((slots, D), F32), dmt=((D, slots), BF),
        dh=((slots, D), BF),
    )
    scratch.update({"q_" + k: cross[k] for k in CROSS})
    scratch.update(
        b3_cross=((3, 1, D), F32),
        bup_cross=((1, FF), F32),
        gain=((2, 1, D), F32),
        gain_cross=((2, 1, D), F32),
        bt=((4, 1, D), F32),
        bt_cross=((4, 1, D), F32),
        x_bqv=((2, 2, HALF_D), F32),
        x_bup=((2, HALF_FF), F32),
        cot=((rows, D), BF),
        dmt=((D, rows), BF),
        ring_w=((4, D, D), BF),
        act_first=((segs, FF), F32),
        cot_all=((dp, segs, D), BF),
        cls_all=((dp, segs, D), BF),
        hat_all=((dp, segs, D + SEG), F32),
        act_all=((dp, segs, FF), BF),
        rows64=((total_segs, D), F32),
        hat64=((total_segs, D + SEG), F32),
        act64=((total_segs, FF), F32),
        undeal=((total_segs, slots), BF),
        back=((8, slots), BF),
        allowed=((SEG, SEG), F32),
        ret=((8, D), F32),
        dc=((8, D), F32),
        late=((SEG, D), BF),
        late_t=((D, SEG), BF),
        small=((12, 1, D), F32),
        small1=((20, 1, D), F32),
        small_in=((9, 1, D), F32),
        small1_in=((17, 1, D), F32),
        total=((9, 1, D), F32),
        total_x=((9, 1, D), F32),
        x_small=((9, 1, D), F32),
        y_small=((9, 1, D), F32),
        z_small=((zs, 9, 1, D), F32),
        shard1=((CHUNKS, shard, CHUNK), F32),
        shard_out=((CHUNKS + 4, shard, CHUNK), BF),
        shard_in=((CHUNKS + 4, shard, CHUNK), BF),
        mine=((CHUNKS, shard, CHUNK), F32),
        gbuf=((RING, zs, 2, 2, shard, CHUNK), BF),
        sib_out=((SLOTS, D, CHUNK), BF),
        sib_in=((SLOTS, D, CHUNK), BF),
        one_in=((RING, 2, zs // 2, 2, shard, CHUNK), BF),
        two_in=((RING, 2, zs // 2, shard, CHUNK), BF),
        three_in=((RING, zs - 1, shard, CHUNK), BF),
    )
    dma = pltpu.SemaphoreType.DMA
    sems = dict(
        local_sem=dma((20,)),
        w_send=dma((2, 5)),
        w_recv=dma((2, 5)),
        ring_sem=dma((4, 2)),
        g_send=dma((4, dp)),
        g_recv=dma((4, dp)),
        misc_send=dma((9,)),
        misc_recv=dma((9,)),
        sib_send=dma((SLOTS,)),
        sib_recv=dma((SLOTS,)),
        one_send=dma((CHUNKS, 2)),
        one_recv=dma((CHUNKS, 2)),
        two_send=dma((CHUNKS, 2)),
        two_recv=dma((CHUNKS, 2)),
        three_send=dma((CHUNKS, zs - 1)),
        three_recv=dma((CHUNKS, zs - 1)),
        z_send=dma((zs,)),
        z_recv=dma((zs,)),
        credit=pltpu.SemaphoreType.REGULAR,
    )
    ins = dict(
        seg_doc=smem, doc_len=smem, seg_doc_v=small, tokens=hbm, cotangent=hbm, b_qv=small, b_up=small,
        norm_gain=small, bias_terms=small, seg_pos=small,
        a_wqkv=hbm, a_wout=hbm, a_wup=hbm, a_wdown=hbm,
    )
    names = list(ins) + list(outs) + list(scratch) + list(sems)
    result = pl.pallas_call(
        partial(whole_kernel, dp, names),
        out_shape=arrays(outs),
        in_specs=list(ins.values()),
        out_specs=[hbm, hbm, hbm, small] + [hbm] * 4,
        scratch_shapes=vmem(scratch) + list(sems.values()),
        compiler_params=pltpu.CompilerParams(
            collective_id=0, has_side_effects=True, vmem_limit_bytes=VMEM_LIMIT
        ),
        name="both_layers",
    )(*[inputs[k] for k in ins])
    return dict(zip(outs, result))


VMEM_LIMIT = 64 << 20


def finish_kernel(
    enc, grad, shard, small, o_enc, o_grad, g_qkv, g_out, g_up, g_down, g_bqv, g_bup, g_gain, g_terms, g_pos,
    enc_v, grad_v, shard_v, sems,
):
    copies = Copies(sems)
    loads = [copies.start(grad.at[b], grad_v.at[b]) for b in range(grad.shape[0])]
    load_shard = copies.start(shard, shard_v)
    loads_enc = [copies.start(enc.at[b], enc_v.at[b]) for b in range(enc.shape[0])]
    outs = []
    for b, load in enumerate(loads):
        load.wait()
        outs.append(copies.start(grad_v.at[b], o_grad.at[b]))
    load_shard.wait()
    for layer in range(2):
        for c in range(4):
            lanes = slice(c * CHUNK, (c + 1) * CHUNK)
            outs.append(copies.start(shard_v.at[layer, c], g_down.at[layer, :, lanes]))
            outs.append(copies.start(shard_v.at[layer, 4 + c], g_up.at[layer, :, lanes]))
        outs.append(copies.start(shard_v.at[layer, 8], g_out.at[layer]))
        for k in range(3):
            outs.append(copies.start(shard_v.at[layer, 9 + k], g_qkv.at[layer, QKV_OF[k]]))
    for b, load in enumerate(loads_enc):
        load.wait()
        outs.append(copies.start(enc_v.at[b], o_enc.at[b]))
    for layer in range(2):
        at = 9 * layer
        for k in range(2):
            g_gain[layer, k : k + 1, :] = small[at + k]
            g_bqv[layer, k : k + 1, :] = small[at + 6, :, k * HALF_D : (k + 1) * HALF_D]
            g_bup[layer : layer + 1, k * D : (k + 1) * D] = small[at + 7 + k]
        for k in range(4):
            g_terms[layer, k : k + 1, :] = small[at + 2 + k]
    for k in range(MAXSEG):
        g_pos[k : k + 1, :] = small[18 + k]
    for copy in outs:
        copy.wait()


def fused(tokens, seg_doc, doc_len, w_qkv, b_qv, w_out, w_up, b_up, w_down, norm_gain, bias_terms, seg_pos, cotangent):
    dp = lax.axis_size("dp")
    whole = run_whole(
        dp,
        dict(
            seg_doc=seg_doc, doc_len=doc_len, seg_doc_v=seg_doc, tokens=tokens, cotangent=cotangent,
            b_qv=b_qv, b_up=b_up, norm_gain=norm_gain, bias_terms=bias_terms,
            seg_pos=seg_pos, a_wqkv=w_qkv, a_wout=w_out, a_wup=w_up, a_wdown=w_down,
        ),
    )
    rows = D // dp
    shapes = [
        (2, 3, rows, HALF_D), (2, rows, HALF_D), (2, rows, HALF_FF), (2, rows, HALF_FF),
        (2, 2, HALF_D), (2, HALF_FF), (2, 2, D), (2, 4, D), (MAXSEG, D),
    ]
    hbm = pl.BlockSpec(memory_space=pl.ANY)
    small = pl.BlockSpec(memory_space=pltpu.VMEM)
    results = [whole[k] for k in ("o_enc", "o_grad", "o_shard", "o_small")]
    enc, grad, g_qkv, g_out, g_up, g_down, g_bqv, g_bup, g_gain, g_terms, g_pos = pl.pallas_call(
        finish_kernel,
        out_shape=[jax.ShapeDtypeStruct(a.shape, a.dtype) for a in results[:2]]
        + [jax.ShapeDtypeStruct(shape, F32) for shape in shapes],
        in_specs=[hbm] * 3 + [small],
        out_specs=[hbm] * 6 + [small] * 5,
        scratch_shapes=[pltpu.VMEM(a.shape, a.dtype) for a in results[:3]]
        + [pltpu.SemaphoreType.DMA((40,))],
        compiler_params=pltpu.CompilerParams(vmem_limit_bytes=VMEM_LIMIT),
        name="lay_out",
    )(*results)
    return (
        enc, grad, g_qkv, g_bqv, g_out.transpose(0, 2, 1), g_up, g_bup, g_down.transpose(0, 2, 1),
        g_gain, g_terms, g_pos,
    )


def solution(mesh):
    in_specs = (
        P(None, "dp", None),
        P(),
        P(),
        P(None, None, None, "tensor"),
        P(None, None, "tensor"),
        P(None, "tensor", None),
        P(None, None, "tensor"),
        P(None, "tensor"),
        P(None, "tensor", None),
        P(),
        P(),
        P(),
        P(None, "dp", None),
    )
    out_specs = (
        P(None, "dp", None),
        P(None, "dp", None),
        P(None, None, "dp", "tensor"),
        P(None, None, "tensor"),
        P(None, "tensor", "dp"),
        P(None, "dp", "tensor"),
        P(None, "tensor"),
        P(None, "tensor", "dp"),
        P(),
        P(),
        P(),
    )
    body = fused if mesh.shape["dp"] == 16 and mesh.shape["tensor"] == 2 else local
    return jax.shard_map(body, mesh=mesh, in_specs=in_specs, out_specs=out_specs, check_vma=False)
```

profile of v0, /device:TPU:0, one launch (start us, length us, event | category | flops | bytes accessed | tf_op | source)
XLA Modules:
  0.0 126.0 jit_solution(16195076683819866832)
XLA Ops:
  0.6 118.3 %both_layers.1 = (bf16[2,512,768]{2,1,0:T(8,128)(2,1)}, f32[2,512,768]{2,1,0:T(8,128)}, f32[2,12,48,384]{3,2,1,0:T(8,128)}, f32[26,1,768]{2,1,0:T(1,128)}, bf16[...) custom-call(s32[2,64]{1,0:T(2,128)} %refs_2_.1, ...), custom_call_target="tpu_custom_call" | custom-call | tf_op jit(solution)/shard_map/both_layers/pallas_call | solution.py:1537
  119.0 6.8 %lay_out.1 = (bf16[2,512,768]{2,1,0:T(8,128)(2,1)}, f32[2,512,768]{2,1,0:T(8,128)}, f32[2,3,48,384]{3,2,1,0:T(8,128)}, f32[2,48,384]{2,1,0:T(8,128)}, f32[2,48,1...) custom-call(bf16[2,512,768]{2,1,0:T(8,128)(2,1)} %get-tuple-element., ...), custom_call_target="tpu_custom_call" | custom-call | tf_op jit(solution)/shard_map/lay_out/pallas_call | solution.py:1610
where the time goes:
time: 126 us
  Pallas kernels  125 us (99%)
    pallas_call x1, Pallas kernels, run_whole(): pl.pallas_call(partial(whole_kernel, dp, names), out_shape=arrays(outs),...  118 us
    pallas_call x1, Pallas kernels, fused(): pl.pallas_call(finish_kernel, out_shape=[jax.ShapeDtypeStruct(a.shape, a....  6.85 us

commit v1 on v0

--- a/solution.py
+++ b/solution.py
@@ -736,10 +736,11 @@
 
     def rows_into(self, dest):
         segs = self.everyone.shape[1]
-        pack = 8 // segs
+        tall = 16 if dest.dtype == BF else 8
+        pack = tall // segs
         for i in range(self.dp // pack):
             blocks = [self.everyone[i * pack + k].astype(F32) for k in range(pack)]
-            dest[i * 8 : i * 8 + 8, :] = jnp.concatenate(blocks, axis=0)
+            dest[i * tall : i * tall + tall, :] = jnp.concatenate(blocks, axis=0).astype(dest.dtype)
 
 
 SLOTS = 4
@@ -790,7 +791,7 @@
         + [("down", j) for j in range(4)] * 2
         + [("up", j) for j in range(4)] + [("out", 0)] + [("qkv", c) for c in range(3)]
     )
-    DEPTH = 4
+    DEPTH = 3
 
     def __init__(self, r, arriving):
         self.r = r
@@ -872,7 +873,7 @@
     def back_down_piece(j, w):
         du = (mm_nt(q.dm[...], w[...]) * q.gp[:, lanes(j)].astype(F32)).astype(BF)
         q.gp[:, lanes(j)] = du
-        r.bup_sum[:, lanes(j)] = jnp.sum(du.astype(F32), axis=0, keepdims=True)
+        q.bup_sum[:, lanes(j)] = jnp.sum(du.astype(F32), axis=0, keepdims=True)
 
     for j in range(4):
         stream.take(back_down_piece)
@@ -1000,14 +1001,15 @@
     loads["wout"].wait()
     swaps[0, "wout"].wait_recv()
     attn_out(r)
+    swap(1, "wqkv")
+    swap(1, "wout")
     norm_one(r, r.xb)
     loads["wup"].wait()
     mlp_up(r, lambda j: pl.when(j == 2)(swaps[0, "wup"].wait_recv))
+    swap(1, "wup")
     transpose_into(r.h1t, r.h1b, rows)
     loads["wdown"].wait()
     mlp_down(r, lambda half: pl.when(half == 1)(swaps[0, "wdown"].wait_recv))
-    swap(1, "wqkv")
-    swap(1, "wout")
     norm_two(r, r.y1)
     cls_gather.start(first_of_segments(r.y1, segs).astype(BF))
     hats = first_of_segments(r.xh2, segs)
@@ -1129,7 +1131,7 @@
             for o, copy in enumerate(stage_three(at)):
                 copy.wait_recv()
                 total = total + r.three_in[ring(at), o].astype(F32)
-            r.mine[c] = r.mine[c] + total if c < 4 else total
+            r.mine[c] = r.mine[c] + total if c < 8 else total
             for copy in (*stage_one(at), *stage_two(at), *stage_three(at)):
                 copy.wait_send()
 
@@ -1138,14 +1140,19 @@
     def without_first(s, at):
         return jnp.where(lax.rem(block_row, SEG) == 0, 0.0, r.cot[at, :].astype(F32))
 
-    r.act_first[...] = first_of_segments(r.g, segs)
+    r.act_first[:, 0:FF] = first_of_segments(r.g, segs)
+    r.act_first[:, FF : 2 * FF] = first_of_segments(r.gp, segs)
+    r.act_first[:, 2 * FF :] = first_of_segments(r.h1b, segs)
     r.small_common = r.small
     back_norm_two(r, without_first)
     hooks("down", "other")
-    swap(1, "wup")
     hooks("down", "launch")
     swap(1, "wdown")
     act_gather.start(r.act_first[...].astype(BF))
+    grad_hidden(r)
+    hooks("up", "other")
+    hooks("up", "own")
+    launch(4, 5)
 
     q = Names(
         **{k: getattr(r, "q_" + k) for k in CROSS},
@@ -1156,6 +1163,8 @@
         b3=r.b3_cross,
         bup=r.bup_cross,
         qv_sum=r.qv_sum,
+        bup_sum=r.bup_sum_cross,
+        small=r.small1,
     )
     q.dr, q.dm, q.small_common = q.h1, q.h1b, r.small1
     slots = q.xb.shape[0]
@@ -1188,7 +1197,8 @@
     pick_row = lax.broadcasted_iota(jnp.int32, (8, total_segs), 0)
     pick_seg = lax.broadcasted_iota(jnp.int32, (8, total_segs), 1)
     picked = jnp.logical_and(pick_row < segs, pick_seg == d * segs + pick_row)
-    r.back[...] = mm(jnp.where(picked, 1.0, 0.0).astype(BF), r.undeal[...]).astype(BF)
+    r.pick[...] = jnp.where(picked, 1.0, 0.0).astype(BF)
+    r.back[...] = mm(r.pick[...], r.undeal[...]).astype(BF)
     live = mm_nt(jnp.ones((8, total_segs), BF), deal)[0:1] > 0.5
     key_doc = lax.broadcasted_iota(jnp.int32, (SEG, SEG), 1) >> 3
     row_doc = lax.broadcasted_iota(jnp.int32, (SEG, SEG), 0) >> 3
@@ -1214,15 +1224,18 @@
             r.shard_out[c] = mm(mine, right[:, other_at : other_at + CHUNK]).astype(BF)
 
     def pump(point):
-        if point == "back_up":
+        if point == "up":
             second(0, 1)
+        elif point == "down":
+            second(2, 3)
+            launch(6, 7)
+        elif point == "back_up":
+            second(4, 5)
         elif point == "attend_back":
-            second(2, 3)
+            third(0, 1)
 
     cross_layer(r, q, stream, lambda s: r.allowed[...] > 0.5, pump, cross_hooks)
-    r.small, keep_small = r.small1, r.small
-    pack_halves(r)
-    r.small = keep_small
+    pack_halves(q)
     total = q.dr[0:MAXSEG, :]
     for j in range(1, total_docs):
         total = total + q.dr[j * MAXSEG : (j + 1) * MAXSEG, :]
@@ -1242,7 +1255,6 @@
         out = jnp.where(top, norm_back(grad, hat, r.rs2[at, 0:1], r.gain[1]), 0.0)
         out_low = out.astype(BF)
         r.dr[at, :] = jnp.where(top, out, r.dr[at, :])
-        r.dm[at, :] = jnp.where(top, out_low.astype(F32), r.dm[at, :].astype(F32)).astype(BF)
         gain_sum = gain_sum + jnp.sum(grad * hat, axis=0, keepdims=True)
         shift_sum = shift_sum + jnp.sum(grad, axis=0, keepdims=True)
         low_sum = low_sum + jnp.sum(out_low.astype(F32), axis=0, keepdims=True)
@@ -1263,15 +1275,36 @@
     r.late[0:total_segs, :] = late
     r.late[total_segs:, :] = jnp.zeros((SEG - total_segs, D), BF)
     transpose_into(r.late_t, r.late, SEG)
-    mine = r.late_t[pl.ds(pl.multiple_of(d * shard, 16), shard), 0:total_segs]
-    for c in range(4):
-        for half in range(2):
-            cols = slice(half * HALF_FF + c * CHUNK, half * HALF_FF + (c + 1) * CHUNK)
-            part = mm(mine, r.act64[:, cols].astype(BF))
-            if half == 0:
-                r.mine[c] = part
-            else:
-                r.shard_out[CHUNKS + c] = part.astype(BF)
+    shard_rows = pl.ds(pl.multiple_of(d * shard, 16), shard)
+
+    def late_chunks(low, base):
+        mine = r.late_t[shard_rows, 0:total_segs]
+        for c in range(4):
+            for half in range(2):
+                cols = slice(base + half * HALF_FF + c * CHUNK, base + half * HALF_FF + (c + 1) * CHUNK)
+                part = mm(mine, r.act64[:, cols])
+                if half == 0:
+                    r.mine[low + c] = part
+                else:
+                    r.shard_out[CHUNKS + low + c] = part.astype(BF)
+
+    late_chunks(0, 0)
+
+    @pl.loop(0, 3)
+    def _(j):
+        cols = span(j, 1024)
+        slopes = pl.ds(pl.multiple_of(FF + j * 1024, 1024), 1024)
+        du = (mm_nt(r.late[0:total_segs, :], r.wdown[cols, :]) * r.act64[:, slopes].astype(F32)).astype(BF)
+        r.act64[:, slopes] = du
+        mine = mm(r.pick[...], du)
+        r.bup_sum[:, cols] = r.bup_sum[:, cols] + jnp.sum(mine, axis=0, keepdims=True)
+        for s in range(segs):
+            at = slice(s * SEG, s * SEG + 16)
+            r.gp[at, cols] = jnp.where(top, mine[s : s + 1, :], r.gp[at, cols].astype(F32)).astype(BF)
+
+    r.late[0:total_segs, :] = r.act64[:, 2 * FF :]
+    transpose_into(r.late_t, r.late, SEG)
+    late_chunks(4, FF)
     cross_swap = [
         remote(r.shard_out, r.shard_in, r.misc_send.at[1], r.misc_recv.at[1], sibling),
         remote(r.small1.at[0:6], r.small1_in.at[0:6], r.misc_send.at[2], r.misc_recv.at[2], sibling),
@@ -1280,12 +1313,7 @@
     for copy in cross_swap:
         copy.start()
 
-    third(0, 1)
-    grad_hidden(r)
     third(2, 3)
-    hooks("up", "other")
-    hooks("up", "own")
-    launch(4, 5)
     grad_middle(r)
     for copy in cross_swap:
         copy.wait()
@@ -1296,24 +1324,22 @@
     )
     outs.append(copies.start(r.shard1, r.o_shard.at[1]))
     back_norm_one(r)
-    second(4)
-    launch(6)
+    second(6, 7)
     hooks("out", "other")
     grad_heads(r)
     hooks("out", "own")
-    second(5)
-    launch(7)
+    launch(8)
+    third(4, 5)
     attend_back_values(r)
     hooks("v", "other")
     finish(0, 1, 2, 3)
-    for c in range(4):
+    for c in range(8):
         r.mine[c] = r.mine[c] + r.shard_in[CHUNKS + c].astype(F32)
 
     def halfway():
-        second(6)
-        third(4)
         hooks("v", "own")
-        launch(8, 9)
+        launch(9)
+        third(6)
 
     attend_back(r, False, lambda i: pl.when(i == 1)(halfway))
     bias_heads(r)
@@ -1324,27 +1350,31 @@
     ]
     for copy in small_swap:
         copy.start()
+    second(8)
     hooks("qk", "other")
-    second(7)
-    third(5)
+    third(7)
     for copy in small_swap:
         copy.wait()
     r.total[...] = r.small[0:9] + r.small_in[...]
     x_small = remote(r.total, r.x_small, r.misc_send.at[7], r.misc_recv.at[7], x_peer)
     x_small.start()
-    hooks("qk", "own")
-    launch(10, 11)
+    hooks("qk", "own", (10, 11))
+    second(9)
+    launch(10)
+    hooks("qk", "own", (11, 12))
+    launch(11)
     x_small.wait()
     r.total_x[...] = r.total[...] + r.x_small[...]
     y_small = remote(r.total_x, r.y_small, r.misc_send.at[8], r.misc_recv.at[8], y_peer)
     y_small.start()
-    third(6)
-    second(8)
+    third(8)
     grad_input(r)
     grad_swap = remote(r.dr, r.o_grad.at[t], r.misc_send.at[6], r.misc_recv.at[6], sibling)
     grad_swap.start()
     outs.append(copies.start(r.dr, r.o_grad.at[t]))
-    third(7)
+    finish(4, 5, 6)
+    third(9)
+    second(10, 11)
     y_small.wait()
     r.z_small[z] = r.total_x[...] + r.y_small[...]
     z_sends = []
@@ -1353,14 +1383,7 @@
             remote(r.z_small.at[z], r.z_small.at[z], r.z_send.at[o], r.z_recv.at[z], z_peers[o - 1])
         )
         z_sends[-1].start()
-    second(9)
-    finish(4)
-    third(8)
-    second(10)
-    finish(5)
-    third(9)
-    second(11)
-    finish(6, 7)
+    finish(7)
     third(10)
     for o in range(1, zs):
         source = lax.rem(z + o, zs)
@@ -1470,15 +1493,17 @@
         x_bup=((2, HALF_FF), F32),
         cot=((rows, D), BF),
         dmt=((D, rows), BF),
-        ring_w=((4, D, D), BF),
-        act_first=((segs, FF), F32),
+        ring_w=((3, D, D), BF),
+        act_first=((segs, 2 * FF + D), F32),
+        pick=((8, total_segs), BF),
+        bup_sum_cross=((1, FF), F32),
         cot_all=((dp, segs, D), BF),
         cls_all=((dp, segs, D), BF),
         hat_all=((dp, segs, D + SEG), F32),
-        act_all=((dp, segs, FF), BF),
+        act_all=((dp, segs, 2 * FF + D), BF),
         rows64=((total_segs, D), F32),
         hat64=((total_segs, D + SEG), F32),
-        act64=((total_segs, FF), F32),
+        act64=((total_segs, 2 * FF + D), BF),
         undeal=((total_segs, slots), BF),
         back=((8, slots), BF),
         allowed=((SEG, SEG), F32),
@@ -1496,8 +1521,8 @@
         y_small=((9, 1, D), F32),
         z_small=((zs, 9, 1, D), F32),
         shard1=((CHUNKS, shard, CHUNK), F32),
-        shard_out=((CHUNKS + 4, shard, CHUNK), BF),
-        shard_in=((CHUNKS + 4, shard, CHUNK), BF),
+        shard_out=((CHUNKS + 8, shard, CHUNK), BF),
+        shard_in=((CHUNKS + 8, shard, CHUNK), BF),
         mine=((CHUNKS, shard, CHUNK), F32),
         gbuf=((RING, zs, 2, 2, shard, CHUNK), BF),
         sib_out=((SLOTS, D, CHUNK), BF),
@@ -1511,7 +1536,7 @@
         local_sem=dma((20,)),
         w_send=dma((2, 5)),
         w_recv=dma((2, 5)),
-        ring_sem=dma((4, 2)),
+        ring_sem=dma((3, 2)),
         g_send=dma((4, dp)),
         g_recv=dma((4, dp)),
         misc_send=dma((9,)),

time: 126 us -> 124 us (0.984)
  Pallas kernels: 125 us -> 123 us
    pallas_call x1, Pallas kernels: 118 us -> 116 us  [run_whole(): pl.pallas_call(partial(whole_kernel, dp, names), out_shape=arrays(outs),...]
where the time goes in v1:
time: 124 us; the launch traced here: 123 us
  Pallas kernels  123 us (99%)
    pallas_call x1, Pallas kernels, run_whole(): pl.pallas_call(partial(whole_kernel, dp, names), out_shape=arrays(outs),...  116 us
    pallas_call x1, Pallas kernels, fused(): pl.pallas_call(finish_kernel, out_shape=[jax.ShapeDtypeStruct(a.shape, a....  6.85 us

profile of v1, /device:TPU:0, one launch (start us, length us, event | category | flops | bytes accessed | tf_op | source)
XLA Modules:
  0.0 123.5 jit_solution(14264864460130791424)
XLA Ops:
  0.6 115.8 %both_layers.1 = (bf16[2,512,768]{2,1,0:T(8,128)(2,1)}, f32[2,512,768]{2,1,0:T(8,128)}, f32[2,12,48,384]{3,2,1,0:T(8,128)}, f32[26,1,768]{2,1,0:T(1,128)}, bf16[...) custom-call(s32[2,64]{1,0:T(2,128)} %refs_2_.1, ...), custom_call_target="tpu_custom_call" | custom-call | tf_op jit(solution)/shard_map/both_layers/pallas_call | solution.py:1562
  116.4 6.8 %lay_out.1 = (bf16[2,512,768]{2,1,0:T(8,128)(2,1)}, f32[2,512,768]{2,1,0:T(8,128)}, f32[2,3,48,384]{3,2,1,0:T(8,128)}, f32[2,48,384]{2,1,0:T(8,128)}, f32[2,48,1...) custom-call(bf16[2,512,768]{2,1,0:T(8,128)(2,1)} %get-tuple-element., ...), custom_call_target="tpu_custom_call" | custom-call | tf_op jit(solution)/shard_map/lay_out/pallas_call | solution.py:1635

commit v2 on v1

--- a/solution.py
+++ b/solution.py
@@ -593,9 +593,8 @@
 
 
 def grad_middle(r):
-    @pl.loop(0, 2)
-    def _(n):
-        cols = span(n, CHUNK)
+    for n in range(3):
+        cols = slice(n * 256, n * 256 + 256)
         r.dr[:, cols] = r.dr[:, cols] + mm_nt(r.gp[...], r.wup[cols, :])
 
 
@@ -1581,13 +1580,15 @@
     enc_v, grad_v, shard_v, sems,
 ):
     copies = Copies(sems)
-    loads = [copies.start(grad.at[b], grad_v.at[b]) for b in range(grad.shape[0])]
+    quarter = grad.shape[1] // 4
+    pieces = [(b, slice(k * quarter, (k + 1) * quarter)) for b in range(grad.shape[0]) for k in range(4)]
+    loads = [copies.start(grad.at[b, at], grad_v.at[b, at]) for b, at in pieces]
     load_shard = copies.start(shard, shard_v)
     loads_enc = [copies.start(enc.at[b], enc_v.at[b]) for b in range(enc.shape[0])]
     outs = []
-    for b, load in enumerate(loads):
+    for (b, at), load in zip(pieces, loads):
         load.wait()
-        outs.append(copies.start(grad_v.at[b], o_grad.at[b]))
+        outs.append(copies.start(grad_v.at[b, at], o_grad.at[b, at]))
     load_shard.wait()
     for layer in range(2):
         for c in range(4):
@@ -1639,7 +1640,7 @@
         in_specs=[hbm] * 3 + [small],
         out_specs=[hbm] * 6 + [small] * 5,
         scratch_shapes=[pltpu.VMEM(a.shape, a.dtype) for a in results[:3]]
-        + [pltpu.SemaphoreType.DMA((40,))],
+        + [pltpu.SemaphoreType.DMA((56,))],
         compiler_params=pltpu.CompilerParams(vmem_limit_bytes=VMEM_LIMIT),
         name="lay_out",
     )(*results)

time: 124 us -> 124 us (level)
  no operation moved by 1% of the time
where the time goes in v2:
time: 124 us
  Pallas kernels  123 us (99%)
    pallas_call x1, Pallas kernels, run_whole(): pl.pallas_call(partial(whole_kernel, dp, names), out_shape=arrays(outs),...  116 us
    pallas_call x1, Pallas kernels, fused(): pl.pallas_call(finish_kernel, out_shape=[jax.ShapeDtypeStruct(a.shape, a....  7.31 us

profile of v2, /device:TPU:0, one launch (start us, length us, event | category | flops | bytes accessed | tf_op | source)
XLA Modules:
  0.0 124.1 jit_solution(8013719118343618549)
XLA Ops:
  0.6 115.9 %both_layers.1 = (bf16[2,512,768]{2,1,0:T(8,128)(2,1)}, f32[2,512,768]{2,1,0:T(8,128)}, f32[2,12,48,384]{3,2,1,0:T(8,128)}, f32[26,1,768]{2,1,0:T(1,128)}, bf16[...) custom-call(s32[2,64]{1,0:T(2,128)} %refs_2_.1, ...), custom_call_target="tpu_custom_call" | custom-call | tf_op jit(solution)/shard_map/both_layers/pallas_call | solution.py:1561
  116.6 7.3 %lay_out.1 = (bf16[2,512,768]{2,1,0:T(8,128)(2,1)}, f32[2,512,768]{2,1,0:T(8,128)}, f32[2,3,48,384]{3,2,1,0:T(8,128)}, f32[2,48,384]{2,1,0:T(8,128)}, f32[2,48,1...) custom-call(bf16[2,512,768]{2,1,0:T(8,128)(2,1)} %get-tuple-element., ...), custom_call_target="tpu_custom_call" | custom-call | tf_op jit(solution)/shard_map/lay_out/pallas_call | solution.py:1636
